TPU v7x, 32 devices: a whole 2x2x4 slice. The times are simulated.
32 devices in a mesh: dp: 4 (over z), space: 8 (over y, x, core).
Axes of the slice: x: 2, y: 2, z: 4, core: 2. Of those that a mesh axis runs over, the one named last changes fastest.
Arguments:
- features: bfloat16 [4, 256, 64, 256], P('dp', 'space'), may hold values from -6 to 6
- saved: bfloat16 [3, 4, 256, 64, 256], P(None, 'dp', 'space'), may hold values from -6 to 6
- upstream: bfloat16 [3, 4, 256, 64, 256], P(None, 'dp', 'space'), may hold values from -6 to 6
- weight: bfloat16 [3, 3, 3, 256, 256], replicated, may hold values from -0.125 to 0.125
- gain: float32 [3, 256], replicated, may hold values from 0.1 to 1.9
- extent: int32 [4, 8], P('dp', 'space'), may hold values from 1 to 32, 160 in all within a row
Outputs:
- input_grad: bfloat16 [4, 256, 64, 256], P('dp', 'space')
- kernel_grad: float32 [3, 3, 3, 256, 256], replicated
Inputs may be any that keep to these rules, and one draw needn't show every extreme that they name: `extent`: each scene's 8 tile extents sum to 160; some tile of each scene is wholly foreground.
All inputs are finite; a program needn't handle non-finite values. No bound on the sum of `extent` on one device may be relied on, other than what follows from the above.
Results may differ from a plain program's by a relative error of at most 0.00085.
The roundings to bfloat16 on the way count: a program that leaves them out, or rounds other values in their place, can miss the bound.
Values may be sent and summed in bfloat16 or wider, within the bound.
A program may use at most 192 MiB of HBM per device.

v0:
```python
import jax
import jax.numpy as jnp
from jax import lax
from jax.sharding import PartitionSpec as P

kernel_reach = 18
dilation_rates = (6, 12, 18)


def padded(array, sides, width):
    for axis, dim in sides:
        count, length = (lax.axis_size(axis), array.shape[dim])
        up = [(i, (i + 1) % count) for i in range(count - 1)]
        down = [(j, i) for i, j in up]
        last = lax.slice_in_dim(array, length - width, length, axis=dim)
        first = lax.slice_in_dim(array, 0, width, axis=dim)
        before = lax.ppermute(last, axis, up)
        after = lax.ppermute(first, axis, down)
        array = jnp.concatenate([before, array, after], axis=dim)
    return array


def kernel_points(padded_input, dilation_step, border_margin, row_total, column_total, sign_factor):
    pieces = []
    for kernel_row in range(3):
        for kernel_column in range(3):
            top_offset = border_margin + sign_factor * dilation_step * (kernel_row - 1)
            left_offset = border_margin + sign_factor * dilation_step * (kernel_column - 1)
            pieces.append(
                padded_input[
                    top_offset : top_offset + row_total, left_offset : left_offset + column_total, :
                ]
            )
    chans = padded_input.shape[-1]
    return jnp.concatenate(pieces, axis=-1).reshape(row_total * column_total, 9 * chans)


def body(features, saved, upstream, weight, gain, extent):
    row_total, column_total, chans = (features.shape[1], features.shape[2], features.shape[3])
    pixels = row_total * column_total
    limit = extent[0, 0]
    rowid = lax.broadcasted_iota(jnp.int32, (1, row_total, 1, 1), 1)
    inside = (rowid < limit).astype(jnp.float32)
    count = limit.astype(jnp.float32) * column_total
    values = saved[:, 0].astype(jnp.float32)
    masked = values * inside
    counts = jnp.full((3, chans), count, jnp.float32)
    total, first_sum, second_sum = lax.psum(
        (counts, jnp.sum(masked, axis=(1, 2)), jnp.sum(masked * masked, axis=(1, 2))),
        ("dp", "space"),
    )
    mean = first_sum / total
    variance = second_sum / total - mean * mean
    rstd = 1.0 / jnp.sqrt(variance + 1e-05)
    yhat = (values - mean[:, None, None, :]) * rstd[:, None, None, :]
    scaled = gain[:, None, None, :] * upstream[:, 0].astype(jnp.float32) * inside
    first_t, second_t = lax.psum(
        (jnp.sum(scaled, axis=(1, 2)), jnp.sum(scaled * yhat, axis=(1, 2))), ("dp", "space")
    )
    grads = (
        inside
        * rstd[:, None, None, :]
        * (
            scaled
            - (first_t / total)[:, None, None, :]
            - yhat * (second_t / total)[:, None, None, :]
        )
    )
    grads = grads.astype(jnp.bfloat16)
    reversed_kernel = jnp.transpose(weight, (0, 1, 2, 4, 3)).reshape(3, 9 * chans, chans)
    padded_gradients = []
    border_margins = []
    extended = padded(grads, (("space", 1),), kernel_reach)
    for kernel_size in range(3):
        padded_gradients.append(
            jnp.pad(extended[kernel_size], ((0, 0), (kernel_reach, kernel_reach), (0, 0)))
        )
        border_margins.append(kernel_reach)
    input_ext = padded(features[0], (("space", 0),), kernel_reach)
    input_padding = jnp.pad(input_ext, ((0, 0), (kernel_reach, kernel_reach), (0, 0)))
    output_tile = jnp.zeros((pixels, chans), jnp.float32)
    kernels = []
    for kernel_size in range(3):
        dilation_step = dilation_rates[kernel_size]
        gradient_columns = kernel_points(
            padded_gradients[kernel_size],
            dilation_step,
            border_margins[kernel_size],
            row_total,
            column_total,
            -1,
        )
        output_tile = output_tile + jnp.dot(
            gradient_columns, reversed_kernel[kernel_size], preferred_element_type=jnp.float32
        )
        input_columns = kernel_points(
            input_padding, dilation_step, kernel_reach, row_total, column_total, 1
        )
        part = lax.dot_general(
            input_columns,
            grads[kernel_size].reshape(pixels, chans),
            (((0,), (0,)), ((), ())),
            preferred_element_type=jnp.float32,
        )
        part = part.reshape(3, 3, chans, chans)
        kernels.append(part)
    kernel_grad = lax.psum(jnp.stack(kernels), ("dp", "space"))
    input_grad = output_tile.astype(jnp.bfloat16).reshape(1, row_total, column_total, chans)
    return (input_grad, kernel_grad)


def solution(mesh):
    return jax.shard_map(
        body,
        mesh=mesh,
        in_specs=(
            P("dp", "space", None, None),
            P(None, "dp", "space", None, None),
            P(None, "dp", "space", None, None),
            P(),
            P(),
            P("dp", "space"),
        ),
        out_specs=(P("dp", "space", None, None), P()),
        check_vma=False,
    )
```

profile of v0, /device:TPU:0, one launch (start us, length us, event | category | flops | bytes accessed | tf_op | source)
XLA Modules:
  0.0 449.1 jit_solution(5530126332109684079)
XLA Ops:
  9.6 3.2 collective-permute-start.2
  14.8 3.0 fusion.3
  17.8 46.2 %all-reduce.5 = (f32[3,256]{1,0:T(4,128)S(1)}, f32[3,256]{1,0:T(4,128)S(1)}, f32[3,256]{1,0:T(4,128)S(1)}) all-reduce(f32[3,256]{1,0:T(4,128)S(1)} %get-tuple-element.5, f32[3,256]{1,0:T(4,128)S(1)} %broadcast_in_dim.2, f32[3,256]{1,0:T(4,128)S(1)} %get-tuple-element.4), channel_id=1, replica_groups=mesh['dp'=4,'space'=8] {'dp','space'}, use_global_device_ids=true, to_apply=%region_4.0 | all-reduce | flops 2304 | bytes 18432 | tf_op jit(solution)/shard_map/psum | solution.py:48
  64.2 4.7 %fusion.13 = (f32[3,256]{1,0:T(4,128)S(1)}, f32[3,256]{1,0:T(4,128)S(1)}) fusion(bf16[3,1,32,64,256]{4,3,2,1,0:T(8,128)(2,1)} %param.8, f32[3,256]{1,0:T(4,128)} %param.10, f32[32]{0:T(128)S(1)} %compare_convert_fusion, f32[3,256]{1,0:T(4,128)S(1)} %get-tuple-element.11, f32[3,256]{1,0:T(4,128)S(1)} %get-tuple-element.12, bf16[3,1,32,64,256]{4,3,2,1,0:T(8,128)(2,1)} %param.7), kind=kLoop, calls=%fused_computation.20 | loop fusion | flops 14154240 | bytes 6306944 | tf_op jit(solution)/shard_map/reduce_sum | solution.py:58
  68.9 39.3 %all-reduce.4 = (f32[3,256]{1,0:T(4,128)S(1)}, f32[3,256]{1,0:T(4,128)S(1)}) all-reduce(f32[3,256]{1,0:T(4,128)S(1)} %get-tuple-element.3, f32[3,256]{1,0:T(4,128)S(1)} %get-tuple-element.2), channel_id=1, replica_groups=mesh['dp'=4,'space'=8] {'dp','space'}, use_global_device_ids=true, to_apply=%region_8.0 | all-reduce | flops 1536 | bytes 12288 | tf_op jit(solution)/shard_map/psum | solution.py:57
  108.2 4.2 fusion.10
  121.0 6.0 %copy.37 = bf16[3,3,3,256,256]{3,4,2,1,0:T(8,128)(2,1)} copy(bf16[3,3,3,256,256]{4,3,2,1,0:T(8,128)(2,1)} %param.9) | data formatting | bytes 7077888 | tf_op args[3]
  127.0 3.8 fusion.25
  130.8 2.5 fusion.18
  133.3 10.4 %fusion.24 = (bf16[32,64,256]{2,1,0:T(8,128)(2,1)}, bf16[32,64,256]{2,1,0:T(8,128)(2,1)}, bf16[32,64,256]{2,1,0:T(8,128)(2,1)}, bf16[32,64,256]{2,1,0:T(8,128)(2...) fusion(bf16[68,100,256]{2,1,0:T(8,128)(2,1)S(1)} %fusion.18), kind=kLoop, calls=%fused_computation.132 | loop fusion | bytes 37748736 | tf_op jit(solution)/shard_map/slice | solution.py:30
  148.3 5.3 %fusion.21 = (bf16[32,64,256]{2,1,0:T(8,128)(2,1)}, bf16[32,64,256]{2,1,0:T(8,128)(2,1)}, bf16[32,64,256]{2,1,0:T(8,128)(2,1)}, bf16[32,64,256]{2,1,0:T(8,128)(2...) fusion(bf16[32,64,256]{2,1,0:T(8,128)(2,1)} %bitcast.125, ...), kind=kLoop, calls=%fused_computation.62 | loop fusion | flops 3145728 | bytes 8519680 | tf_op jit(solution)/shard_map/concatenate | solution.py:19
  247.5 5.4 %pad_maximum_fusion.4 = (bf16[1,32,64,256]{3,2,1,0:T(8,128)(2,1)}, bf16[1,32,64,256]{3,2,1,0:T(8,128)(2,1)}, bf16[1,32,64,256]{3,2,1,0:T(8,128)(2,1)}, bf16[1,32...) fusion(bf16[3,32,64,256]{3,2,1,0:T(8,128)(2,1)S(1)} %fusion.10,, ...), kind=kLoop, calls=%fused_computation.67 | loop fusion | flops 3145728 | bytes 19267584 | tf_op jit(solution)/shard_map/concatenate | solution.py:19
  253.0 2.7 convolution_bitcast_fusion.2
  257.3 2.7 convolution_bitcast_fusion.1
  260.0 5.2 %convolution_bitcast_fusion = f32[1,3,3,256,256]{4,3,2,1,0:T(8,128)S(1)} fusion(bf16[3,3,256,2048]{3,2,1,0:T(8,128)(2,1)} %bitcast.192, bf16[2048,256,1,1]{1,0,3,2:T(8,128)(2,1)S(1)} %bitcast.141), kind=kOutput, calls=%fused_computation.58 | convolution fusion | flops 2415919104 | bytes 12845056 | tf_op jit(solution)/shard_map/dot_general | solution.py:99
  265.3 3.4 pad_maximum_fusion
  268.7 3.0 pad_maximum_fusion.1
  272.8 6.2 %pad_slice_fusion = (bf16[32,64,256]{2,1,0:T(8,128)(2,1)S(1)}, bf16[32,64,256]{2,1,0:T(8,128)(2,1)S(1)}, bf16[32,64,256]{2,1,0:T(8,128)(2,1)S(1)}, bf16[32,64,25...) fusion(bf16[68,64,256]{2,1,0:T(8,128)(2,1)S(1)} %get-tuple-elem, ...), kind=kLoop, calls=%fused_computation.21 | loop fusion | bytes 17039360 | tf_op jit(solution)/shard_map/slice | solution.py:30
  281.3 5.0 %pad_slice_fusion.12 = (bf16[32,64,256]{2,1,0:T(8,128)(2,1)S(1)}, bf16[32,64,256]{2,1,0:T(8,128)(2,1)S(1)}, bf16[32,64,256]{2,1,0:T(8,128)(2,1)S(1)}, bf16[32,64...) fusion(bf16[68,64,256]{2,1,0:T(8,128)(2,1)S(1)} %get-tuple-element.15), kind=kLoop, calls=%fused_computation.33 | loop fusion | bytes 8519680 | tf_op jit(solution)/shard_map/slice | solution.py:30
  297.9 2.6 fusion.28
  300.6 2.6 convolution_add_fusion.1
  303.3 3.6 fusion.19
  306.9 128.3 %all-reduce.8.cloned.1.call-done = f32[3,3,3,256,256]{4,3,2,1,0:T(8,128)} async-done(((f32[3,3,3,256,256]{4,3,2,1,0:T(8,128)}), f32[3,3,3,256,256]{4,3,2,1,0:T(8,128)}) %all-reduce.8.cloned.1.call-update) | async-done | bytes 7077904 | tf_op jit(solution)/shard_map/psum | solution.py:107
  435.1 6.7 %copy.118 = f32[3,3,3,256,256]{4,3,2,1,0:T(8,128)} copy(f32[3,3,3,256,256]{4,3,2,1,0:T(8,128)} %all-reduce.8.cloned.1.call-done) | data formatting | bytes 14155776
  (177 shorter events, 127.1 us)
Async XLA Ops:
  7.2 101.0 %copy-start.27 = (f32[3,256]{1,0:T(4,128)S(1)}, f32[3,256]{1,0:T(4,128)}, u32[]{:S(2)}) copy-start(f32[3,256]{1,0:T(4,128)} %param.10) | copy-start | bytes 9220
  7.2 428.0 %all-reduce.8.cloned.1.call-start = ((), (), s32[]{:S(2)}) async-start(), calls=%async_computation | async-start | bytes 14155776 | tf_op jit(solution)/shard_map/psum | solution.py:107
  9.6 121.2 %collective-permute-start.2 = (bf16[18,64,256]{2,1,0:T(8,128)(2,1)}, bf16[18,64,256]{2,1,0:T(8,128)(2,1)}, u32[]{:S(2)}, u32[]{:S(2)}) collective-permute-start(bf16[18,64,256]{2,1,0:T(8,128)(2,1)} %get-tuple-element.81), channel_id=1, source_target_pairs={{0,1},{1,2},{2,3},{3,4},{4,5},{5,6},{6,7},{8,9},{9,10},{10,11},{11... | collective-permute-start | bytes 1769480 | tf_op jit(solution)/shard_map/ppermute | solution.py:17
  12.9 117.9 %collective-permute-start.3 = (bf16[18,64,256]{2,1,0:T(8,128)(2,1)}, bf16[18,64,256]{2,1,0:T(8,128)(2,1)}, u32[]{:S(2)}, u32[]{:S(2)}) collective-permute-start(bf16[18,64,256]{2,1,0:T(8,128)(2,1)} %get-tuple-element.82), channel_id=1, source_target_pairs={{1,0},{2,1},{3,2},{4,3},{5,4},{6,5},{7,6},{9,8},{10,9},{11,10},{12... | collective-permute-start | bytes 1769480 | tf_op jit(solution)/shard_map/ppermute | solution.py:18
  114.8 132.7 %collective-permute-start = (bf16[3,18,64,256]{3,2,1,0:T(8,128)(2,1)}, bf16[3,18,64,256]{3,2,1,0:T(8,128)(2,1)}, u32[]{:S(2)}, u32[]{:S(2)}) collective-permute-start(bf16[3,18,64,256]{3,2,1,0:T(8,128)(2,1)} %get-tuple-element.49), channel_id=1, source_target_pairs={{0,1},{1,2},{2,3},{3,4},{4,5},{5,6},{6,7},{8,9},{9,10},{10,11},{11... | collective-permute-start | bytes 5308424 | tf_op jit(solution)/shard_map/ppermute | solution.py:17
  117.3 130.2 %collective-permute-start.1 = (bf16[3,18,64,256]{3,2,1,0:T(8,128)(2,1)}, bf16[3,18,64,256]{3,2,1,0:T(8,128)(2,1)}, u32[]{:S(2)}, u32[]{:S(2)}) collective-permute-start(bf16[3,18,64,256]{3,2,1,0:T(8,128)(2,1)} %get-tuple-element.50), channel_id=1, source_target_pairs={{1,0},{2,1},{3,2},{4,3},{5,4},{6,5},{7,6},{9,8},{10,9},{11,10},{12... | collective-permute-start | bytes 5308424 | tf_op jit(solution)/shard_map/ppermute | solution.py:18
  194.6 12.0 %copy-start.15 = (bf16[2048,256]{0,1:T(8,128)(2,1)S(1)}, bf16[2048,256]{0,1:T(8,128)(2,1)}, u32[]{:S(2)}) copy-start(bf16[2048,256]{0,1:T(8,128)(2,1)} %copy.50) | copy-start | bytes 3145732
  194.6 13.0 %copy-start.17 = (bf16[2048,256]{0,1:T(8,128)(2,1)S(1)}, bf16[2048,256]{0,1:T(8,128)(2,1)}, u32[]{:S(2)}) copy-start(bf16[2048,256]{0,1:T(8,128)(2,1)} %copy.57) | copy-start | bytes 3145732
  194.6 14.1 %copy-start.18 = (bf16[2048,256]{0,1:T(8,128)(2,1)S(1)}, bf16[2048,256]{0,1:T(8,128)(2,1)}, u32[]{:S(2)}) copy-start(bf16[2048,256]{0,1:T(8,128)(2,1)} %copy.58) | copy-start | bytes 3145732
  194.6 15.2 %copy-start.16 = (bf16[2048,256]{0,1:T(8,128)(2,1)S(1)}, bf16[2048,256]{0,1:T(8,128)(2,1)}, u32[]{:S(2)}) copy-start(bf16[2048,256]{0,1:T(8,128)(2,1)} %copy.59) | copy-start | bytes 3145732
  194.6 16.2 %copy-start.21 = (bf16[2048,256]{0,1:T(8,128)(2,1)S(1)}, bf16[2048,256]{0,1:T(8,128)(2,1)}, u32[]{:S(2)}) copy-start(bf16[2048,256]{0,1:T(8,128)(2,1)} %copy.42) | copy-start | bytes 3145732
  199.3 13.5 %copy-start.22 = (bf16[2048,256]{0,1:T(8,128)(2,1)S(1)}, bf16[2048,256]{0,1:T(8,128)(2,1)}, u32[]{:S(2)}) copy-start(bf16[2048,256]{0,1:T(8,128)(2,1)} %copy.43) | copy-start | bytes 3145732
  199.3 13.5 %copy-start.23 = (bf16[2048,256]{0,1:T(8,128)(2,1)S(1)}, bf16[2048,256]{0,1:T(8,128)(2,1)}, u32[]{:S(2)}) copy-start(bf16[2048,256]{0,1:T(8,128)(2,1)} %copy.52) | copy-start | bytes 3145732
  204.1 10.3 %copy-start.14 = (bf16[2048,256]{0,1:T(8,128)(2,1)S(1)}, bf16[2048,256]{0,1:T(8,128)(2,1)}, u32[]{:S(2)}) copy-start(bf16[2048,256]{0,1:T(8,128)(2,1)} %copy.44) | copy-start | bytes 3145732
  206.5 8.9 %copy-start.13 = (bf16[2048,256]{0,1:T(8,128)(2,1)S(1)}, bf16[2048,256]{0,1:T(8,128)(2,1)}, u32[]{:S(2)}) copy-start(bf16[2048,256]{0,1:T(8,128)(2,1)} %copy.45) | copy-start | bytes 3145732
  207.6 9.0 %copy-start.12 = (bf16[2048,256]{0,1:T(8,128)(2,1)S(1)}, bf16[2048,256]{0,1:T(8,128)(2,1)}, u32[]{:S(2)}) copy-start(bf16[2048,256]{0,1:T(8,128)(2,1)} %copy.46) | copy-start | bytes 3145732
  233.7 11.7 %copy-start.19 = (bf16[2048,256]{0,1:T(8,128)(2,1)S(1)}, bf16[2048,256]{0,1:T(8,128)(2,1)}, u32[]{:S(2)}) copy-start(bf16[2048,256]{0,1:T(8,128)(2,1)} %copy.63) | copy-start | bytes 3145732
  233.7 12.7 %copy-start.20 = (bf16[2048,256]{0,1:T(8,128)(2,1)S(1)}, bf16[2048,256]{0,1:T(8,128)(2,1)}, u32[]{:S(2)}) copy-start(bf16[2048,256]{0,1:T(8,128)(2,1)} %copy.64) | copy-start | bytes 3145732
  247.5 8.6 %slice-start.6 = ((s8[9437184]{0:T(1024)(128)(4,1)}), s8[4194304]{0:T(1024)(128)(4,1)S(1)}, s32[]{:S(2)}) async-start(s8[9437184]{0:T(1024)(128)(4,1)} %bitcast.189), calls=%async_computation.7 | async-start | bytes 8388608
  247.5 9.8 %slice-start.7 = ((s8[9437184]{0:T(1024)(128)(4,1)}), s8[4194304]{0:T(1024)(128)(4,1)S(1)}, s32[]{:S(2)}) async-start(s8[9437184]{0:T(1024)(128)(4,1)} %bitcast.189), calls=%async_computation.8 | async-start | bytes 8388608
  280.1 9.7 %copy-start.10 = (bf16[1,32,64,256]{3,2,1,0:T(8,128)(2,1)S(1)}, bf16[1,32,64,256]{3,2,1,0:T(8,128)(2,1)}, u32[]{:S(2)}) copy-start(bf16[1,32,64,256]{3,2,1,0:T(8,128)(2,1)} %copy-done.9) | copy-start | bytes 3145732
  281.3 14.4 %slice-start.3 = ((s8[9437184]{0:T(1024)(128)(4,1)}), s8[1048576]{0:T(1024)(128)(4,1)S(1)}, s32[]{:S(2)}) async-start(s8[9437184]{0:T(1024)(128)(4,1)} %bitcast.187), calls=%async_computation.4 | async-start | bytes 2097152
  286.3 9.4 %copy-start.7 = (bf16[1,32,64,256]{3,2,1,0:T(8,128)(2,1)S(1)}, bf16[1,32,64,256]{3,2,1,0:T(8,128)(2,1)}, u32[]{:S(2)}) copy-start(bf16[1,32,64,256]{3,2,1,0:T(8,128)(2,1)} %get-tuple-element.46) | copy-start | bytes 3145732
  286.3 9.4 %slice-start.4 = ((s8[9437184]{0:T(1024)(128)(4,1)}), s8[4194304]{0:T(1024)(128)(4,1)S(1)}, s32[]{:S(2)}) async-start(s8[9437184]{0:T(1024)(128)(4,1)} %bitcast.187), calls=%async_computation.5 | async-start | bytes 8388608
  (21 other events, 90.9 us)
Sparse Core Ops, SparseCore 0:
  268.8 166.2 all-reduce.7
where the time goes:
time: 456 us; the launch traced here: 449 us
  local copies, waits for them, and re-layouts  160 us (35%)
  waiting for transfers between devices  128 us (28%)
  blocking collectives  85.5 us (19%)
  other arithmetic  31.7 us (7%)
  matrix products  19.6 us (4%)
  between operations  15.7 us (3%)
  starting transfers between devices  8.5 us (2%)
    psum x1, waiting for transfers between devices, body(): kernel_grad = lax.psum(jnp.stack(kernels), ('dp', 'space'))  128 us
    unnamed x127, local copies, waits for them, and re-layouts  66 us
    concatenate x31, local copies, waits for them, and re-layouts, kernel_points(): jnp.concatenate(pieces, axis=-1)  62.6 us
    psum x1, blocking collectives, body(): lax.psum((counts, jnp.sum(masked, axis=(1, 2)), jnp.sum(masked * masked,...  46.2 us
    psum x1, blocking collectives, body(): lax.psum((jnp.sum(scaled, axis=(1, 2)), jnp.sum(scaled * yhat, axis=(1, 2...  39.3 us
    slice x3, local copies, waits for them, and re-layouts, kernel_points(): padded_input[top_offset:top_offset + row_total, left_offset:left_offset +...  21.6 us
    concatenate x4, other arithmetic, padded(): array = jnp.concatenate([before, array, after], axis=dim)  16.2 us
    dot_general x3, matrix products, body(): lax.dot_general(input_columns, grads[kernel_size].reshape(pixels, chans),...  10.7 us
  transfers between devices with their start and end apart: 5, of which 1 were waited for; matrix products, arithmetic and copies ran while one was open for 40% of the time, Pallas kernels for 0%

commit v1 on v0

v1 whole, which is shorter than its diff:
```python
import functools

import jax
import jax.numpy as jnp
from jax import lax
from jax.experimental import pallas as pl
from jax.experimental.pallas import tpu as pltpu
from jax.sharding import PartitionSpec as P

RATES = (6, 12, 18)
REACH = 18
STARTS = (0, 6, 18)
BOTH = 36
F32 = jnp.float32
BF16 = jnp.bfloat16


def local_stats(cols, ext_ref, saved_ref, up_ref, gain_ref, out_ref):
    limit = ext_ref[0, 0]
    chans = saved_ref.shape[-1]
    pivot = saved_ref[0, 0:16, :].astype(F32)[0:1]

    def fold(x):
        return jnp.sum(x.reshape(cols // 8, 8, chans), axis=0)

    def step(h, carry):
        at = pl.ds(pl.multiple_of(h * cols, cols), cols)
        d = saved_ref[0, at, :].astype(F32) - pivot
        u = up_ref[0, at, :].astype(F32)
        a, b, c, e = carry
        return (a + fold(d), b + fold(d * d), c + fold(u), e + fold(u * d))

    zero = jnp.zeros((8, chans), F32)
    sums = lax.fori_loop(0, limit, step, (zero, zero, zero, zero))
    d, dd, u, ud = [jnp.sum(x, axis=0, keepdims=True) for x in sums]
    n = jnp.full((1, chans), limit * cols, jnp.int32).astype(F32)
    off = d / n
    gain = gain_ref[...]
    rows = [n * pivot + d, dd - d * off, gain * u, gain * (ud - u * off), n]
    out_ref[...] = jnp.concatenate(rows + [jnp.zeros((3, chans), F32)], axis=0)


def merge(parts):
    n = sum(p[4:5] for p in parts)
    mean = sum(p[0:1] for p in parts) / n
    m2 = jnp.zeros_like(n)
    cross = jnp.zeros_like(n)
    for p in parts:
        gap = p[0:1] / p[4:5] - mean
        m2 = m2 + p[1:2] + p[4:5] * gap * gap
        cross = cross + p[3:4] + p[2:3] * gap
    return mean, n, m2, sum(p[2:3] for p in parts), cross


def exchange(sizes, st_ref, gain_ref, out_ref, buf_a, buf_b, mid, send_a, recv_a, send_b, recv_b):
    barrier = pltpu.get_barrier_semaphore()
    for axis, count in sizes:
        me = lax.axis_index(axis)
        for k in range(1, count):
            pl.semaphore_signal(
                barrier, inc=1, device_id={axis: lax.rem(me + k, count)},
                device_id_type=pl.DeviceIdType.MESH,
            )
    pl.semaphore_wait(barrier, sum(count - 1 for _, count in sizes))

    def spread(axis, count, src, buf, send, recv):
        me = lax.axis_index(axis)
        copies = []
        for k in range(1, count):
            copies.append(pltpu.make_async_remote_copy(
                src_ref=src, dst_ref=buf.at[k - 1], send_sem=send.at[k - 1], recv_sem=recv.at[k - 1],
                device_id={axis: lax.rem(me + k, count)}, device_id_type=pl.DeviceIdType.MESH,
            ))
        for copy in copies:
            copy.start()
        for copy in copies:
            copy.wait()
        return merge([src[...]] + [buf[k] for k in range(count - 1)])

    mean, n, m2, s1, cross = spread(*sizes[0], st_ref, buf_a, send_a, recv_a)
    pad = jnp.zeros((3, n.shape[1]), F32)
    mid[...] = jnp.concatenate([mean * n, m2, s1, cross, n, pad], axis=0)
    mean, n, m2, s1, cross = spread(*sizes[1], mid, buf_b, send_b, recv_b)
    rstd = 1.0 / jnp.sqrt(m2 / n + 1e-05)
    slope = rstd * (rstd * (rstd * cross / n))
    rows = [gain_ref[...] * rstd, slope, rstd * (s1 / n), mean]
    out_ref[...] = jnp.concatenate(rows + [jnp.zeros((4, n.shape[1]), F32)], axis=0)


def shifted(g, dx, cols):
    if dx == 0:
        return g
    w = lax.broadcasted_iota(jnp.int32, g.shape, 0)
    keep = (w >= dx) if dx > 0 else (w < cols + dx)
    return jnp.where(keep, pltpu.roll(g, dx % cols, axis=0), 0.0)


def gradients(cols, rows, ext_ref, saved_ref, up_ref, coef_ref, out_ref, top_ref, bottom_ref):
    limit = ext_ref[0, 0]
    branch = pl.program_id(0)
    coef = coef_ref[...]
    a, b, c, mean = coef[0:1], coef[1:2], coef[2:3], coef[3:4]
    for k, rate in enumerate(RATES):

        @pl.when(branch == k)
        def _():
            def step(h, _):
                at = pl.ds(pl.multiple_of(h * cols, cols), cols)
                v = saved_ref[0, at, :].astype(F32)
                u = up_ref[0, at, :].astype(F32)
                g = a * u - c - b * (v - mean)
                g = jnp.where(h < limit, g, 0.0)
                for j in range(3):
                    out_ref[0, j, at, :] = shifted(g, rate * (j - 1), cols).astype(BF16)
                return 0

            lax.fori_loop(0, rows, step, 0)
            here = pl.ds(STARTS[k] * cols, rate * cols)
            top_ref[here, :] = out_ref[0, 1, 0 : rate * cols, :]
            bottom_ref[here, :] = out_ref[0, 1, (rows - rate) * cols : rows * cols, :]


def kernel_terms(cols, rows, before_ref, own_ref, after_ref, g_ref, out_ref, ft):
    branch, column = pl.program_id(0), pl.program_id(1)

    @pl.when((branch == 0) & (column == 0))
    def _():
        start = 0
        for ref in (before_ref, own_ref, after_ref):
            for k in range(ref.shape[0] // 128):
                ft[:, start : start + 128] = ref[k * 128 : (k + 1) * 128, :].T
                start += 128

    rate = 6 * (branch + 1)
    parts = []
    for i in range(3):
        at = pl.multiple_of((REACH + rate * (i - 1)) * cols, 128)
        parts.append(ft[:, pl.ds(at, rows * cols)])
    got = jnp.dot(jnp.concatenate(parts, axis=0), g_ref[0, 0], preferred_element_type=F32)
    out_ref[0, :, 0] = got.reshape(out_ref.shape[1], out_ref.shape[3], out_ref.shape[4])


def input_terms(cols, rows, before_ref, after_ref, g_ref, w_ref, out_ref, ext, acc):
    branch, column = pl.program_id(0), pl.program_id(1)
    ext[REACH * cols : (REACH + rows) * cols, :] = g_ref[0, 0]
    for k, rate in enumerate(RATES):
        for j in range(3):

            @pl.when((branch == k) & (column == j))
            def _():
                def step(r, _):
                    src = pl.ds(pl.multiple_of((STARTS[k] + r) * cols, cols), cols)
                    up = pl.ds(pl.multiple_of((REACH - rate + r) * cols, cols), cols)
                    down = pl.ds(pl.multiple_of((REACH + rows + r) * cols, cols), cols)
                    dx = rate * (j - 1)
                    ext[up, :] = shifted(before_ref[src, :].astype(F32), dx, cols).astype(BF16)
                    ext[down, :] = shifted(after_ref[src, :].astype(F32), dx, cols).astype(BF16)
                    return 0

                lax.fori_loop(0, rate, step, 0)

    rate = 6 * (branch + 1)
    first = (branch == 0) & (column == 0)
    last = (branch == 2) & (column == 2)
    tile = 512

    def block(m, _):
        here = pl.ds(pl.multiple_of(m * tile, tile), tile)
        total = jnp.where(first, 0.0, acc[here, :])
        for i in range(3):
            at = pl.multiple_of((REACH - rate * (i - 1)) * cols + m * tile, cols)
            total = total + lax.dot_general(
                ext[pl.ds(at, tile), :], w_ref[0, i, 0], (((1,), (1,)), ((), ())),
                preferred_element_type=F32,
            )
        acc[here, :] = total

        @pl.when(last)
        def _():
            out_ref[here, :] = total.astype(BF16)

        return 0

    lax.fori_loop(0, rows * cols // tile, block, 0)


def vmem(shape=None, index=None):
    if shape is None:
        return pl.BlockSpec(memory_space=pltpu.VMEM)
    return pl.BlockSpec(shape, index)


def body(features, saved, upstream, weight, gain, extent):
    rows, cols, chans = features.shape[1:]
    pixels = rows * cols
    n_space, n_dp = lax.axis_size("space"), lax.axis_size("dp")
    smem = pl.BlockSpec(memory_space=pltpu.SMEM)
    limit = pltpu.CompilerParams(vmem_limit_bytes=60 * 1024 * 1024)

    feats = features.reshape(pixels, chans)
    up_pairs = [(i, i + 1) for i in range(n_space - 1)]
    down_pairs = [(j, i) for i, j in up_pairs]
    f_before = lax.ppermute(feats[pixels - REACH * cols :], "space", up_pairs)
    f_after = lax.ppermute(feats[: REACH * cols], "space", down_pairs)

    s = saved.reshape(3, pixels, chans)
    u = upstream.reshape(3, pixels, chans)
    wide = gain.reshape(1, 3 * chans)
    stats = pl.pallas_call(
        functools.partial(local_stats, cols),
        grid=(3,),
        in_specs=[
            smem,
            vmem((1, pixels, chans), lambda b: (b, 0, 0)),
            vmem((1, pixels, chans), lambda b: (b, 0, 0)),
            vmem((1, chans), lambda b: (0, b)),
        ],
        out_specs=vmem((8, chans), lambda b: (0, b)),
        out_shape=jax.ShapeDtypeStruct((8, 3 * chans), F32),
        compiler_params=limit,
    )(extent, s, u, wide)
    coef = pl.pallas_call(
        functools.partial(exchange, (("space", n_space), ("dp", n_dp))),
        in_specs=[vmem(), vmem()],
        out_specs=vmem(),
        out_shape=jax.ShapeDtypeStruct((8, 3 * chans), F32),
        scratch_shapes=[
            pltpu.VMEM((n_space - 1, 8, 3 * chans), F32),
            pltpu.VMEM((n_dp - 1, 8, 3 * chans), F32),
            pltpu.VMEM((8, 3 * chans), F32),
            pltpu.SemaphoreType.DMA((n_space - 1,)),
            pltpu.SemaphoreType.DMA((n_space - 1,)),
            pltpu.SemaphoreType.DMA((n_dp - 1,)),
            pltpu.SemaphoreType.DMA((n_dp - 1,)),
        ],
        compiler_params=pltpu.CompilerParams(collective_id=0, has_side_effects=True),
    )(stats, wide)
    halo = jax.ShapeDtypeStruct((BOTH * cols, chans), BF16)
    grads, top, bottom = pl.pallas_call(
        functools.partial(gradients, cols, rows),
        grid=(3,),
        in_specs=[
            smem,
            vmem((1, pixels, chans), lambda b: (b, 0, 0)),
            vmem((1, pixels, chans), lambda b: (b, 0, 0)),
            vmem((8, chans), lambda b: (0, b)),
        ],
        out_specs=[
            vmem((1, 3, pixels, chans), lambda b: (b, 0, 0, 0)),
            vmem((BOTH * cols, chans), lambda b: (0, 0)),
            vmem((BOTH * cols, chans), lambda b: (0, 0)),
        ],
        out_shape=[jax.ShapeDtypeStruct((3, 3, pixels, chans), BF16), halo, halo],
        compiler_params=limit,
    )(extent, s, u, coef)
    g_before = lax.ppermute(bottom, "space", up_pairs)
    g_after = lax.ppermute(top, "space", down_pairs)
    flops = 2 * 27 * pixels * chans * chans
    cost = pl.CostEstimate(flops=flops, bytes_accessed=20_000_000, transcendentals=0)
    terms = pl.pallas_call(
        functools.partial(kernel_terms, cols, rows),
        grid=(3, 3),
        in_specs=[
            vmem((REACH * cols, chans), lambda b, j: (0, 0)),
            vmem((pixels, chans), lambda b, j: (0, 0)),
            vmem((REACH * cols, chans), lambda b, j: (0, 0)),
            vmem((1, 1, pixels, chans), lambda b, j: (b, j, 0, 0)),
        ],
        out_specs=vmem((1, 3, 1, chans, chans), lambda b, j: (b, 0, j, 0, 0)),
        out_shape=jax.ShapeDtypeStruct((3, 3, 3, chans, chans), F32),
        scratch_shapes=[pltpu.VMEM((chans, pixels + BOTH * cols), BF16)],
        compiler_params=limit,
        cost_estimate=cost,
    )(f_before, feats, f_after, grads)
    kernel_grad = lax.psum(terms, ("dp", "space"))
    out = pl.pallas_call(
        functools.partial(input_terms, cols, rows),
        grid=(3, 3),
        in_specs=[
            vmem((BOTH * cols, chans), lambda b, j: (0, 0)),
            vmem((BOTH * cols, chans), lambda b, j: (0, 0)),
            vmem((1, 1, pixels, chans), lambda b, j: (b, j, 0, 0)),
            vmem((1, 3, 1, chans, chans), lambda b, j: (b, 0, j, 0, 0)),
        ],
        out_specs=vmem((pixels, chans), lambda b, j: (0, 0)),
        out_shape=jax.ShapeDtypeStruct((pixels, chans), BF16),
        scratch_shapes=[
            pltpu.VMEM((pixels + BOTH * cols, chans), BF16),
            pltpu.VMEM((pixels, chans), F32),
        ],
        compiler_params=limit,
        cost_estimate=cost,
    )(g_before, g_after, grads, weight)
    return out.reshape(1, rows, cols, chans), kernel_grad


def solution(mesh):
    return jax.shard_map(
        body,
        mesh=mesh,
        in_specs=(
            P("dp", "space", None, None),
            P(None, "dp", "space", None, None),
            P(None, "dp", "space", None, None),
            P(),
            P(),
            P("dp", "space"),
        ),
        out_specs=(P("dp", "space", None, None), P()),
        check_vma=False,
    )
```

time: 456 us -> 242 us (0.53); the launches traced: 449 us -> 241 us
  local copies, waits for them, and re-layouts: 160 us -> 11.6 us
  blocking collectives: 85.5 us -> 0 us
  Pallas kernels: 0 us -> 67.2 us
  other arithmetic: 31.7 us -> 0 us
  matrix products: 19.6 us -> 0 us
  waiting for transfers between devices: 128 us -> 141 us
    psum x2 -> x0, blocking collectives: 85.5 us -> none  [the longest x1 46.2 us: body(): lax.psum((counts, jnp.sum(masked, axis=(1, 2)), jnp.sum(masked * masked,...]
    pallas_call x0 -> x5, Pallas kernels: none -> 67.2 us  [the longest x1 20.7 us: body(): pl.pallas_call(functools.partial(input_terms, cols, rows), grid=(3, 3), i...]
    concatenate x31 -> x0, local copies, waits for them, and re-layouts: 62.6 us -> none  [kernel_points(): jnp.concatenate(pieces, axis=-1)]
    unnamed x127 -> x12, local copies, waits for them, and re-layouts: 66 us -> 10.2 us
    slice x6 -> x1, local copies, waits for them, and re-layouts: 30.2 us -> 1.32 us  [body(): f_after = lax.ppermute(feats[:REACH * cols], 'space', down_pairs)]
    dot_general x6 -> x0, matrix products: 19.6 us -> none  [the longest x3 10.7 us: body(): lax.dot_general(input_columns, grads[kernel_size].reshape(pixels, chans),...]
    concatenate x4 -> x0, other arithmetic: 16.2 us -> none  [padded(): array = jnp.concatenate([before, array, after], axis=dim)]
    reduce_sum x2 -> x0, other arithmetic: 7.75 us -> none  [the longest x1 4.74 us: body(): jnp.sum(scaled, axis=(1, 2))]
  transfers between devices with their start and end apart: 5 -> 5, of which waited for: 1 -> 3; matrix products, arithmetic and copies ran while one was open for 40% -> 1% of each run, Pallas kernels for 0% -> 22%
where the time goes in v1:
time: 242 us; the launch traced here: 241 us
  waiting for transfers between devices  141 us (58%)
  Pallas kernels  67.2 us (28%)
  between operations  14.8 us (6%)
  local copies, waits for them, and re-layouts  11.6 us (5%)
  starting transfers between devices  6.41 us (3%)
    psum x1, waiting for transfers between devices, body(): kernel_grad = lax.psum(terms, ('dp', 'space'))  135 us
    pallas_call x1, Pallas kernels, body(): pl.pallas_call(functools.partial(input_terms, cols, rows), grid=(3, 3), i...  20.7 us
    pallas_call x1, Pallas kernels, body(): pl.pallas_call(functools.partial(exchange, (('space', n_space), ('dp', n_...  17.3 us
    pallas_call x1, Pallas kernels, body(): pl.pallas_call(functools.partial(kernel_terms, cols, rows), grid=(3, 3),...  14.5 us
    unnamed x12, local copies, waits for them, and re-layouts  10.2 us
    pallas_call x1, Pallas kernels, body(): pl.pallas_call(functools.partial(gradients, cols, rows), grid=(3,), in_sp...  9.28 us
    pallas_call x1, Pallas kernels, body(): pl.pallas_call(functools.partial(local_stats, cols), grid=(3,), in_specs=...  5.42 us
  transfers between devices with their start and end apart: 5, of which 3 were waited for; matrix products, arithmetic and copies ran while one was open for 1% of the time, Pallas kernels for 22%

profile of v1, /device:TPU:0, one launch (start us, length us, event | category | flops | bytes accessed | tf_op | source)
XLA Modules:
  0.0 240.9 jit_solution(3564838621947168217)
XLA Ops:
  7.2 0.0 all-reduce.2.cloned.1.call-start
  7.2 1.3 fusion
  8.5 2.4 %collective-permute-start.2 = (bf16[1152,256]{1,0:T(8,128)(2,1)S(1)}, bf16[1152,256]{1,0:T(8,128)(2,1)S(1)}, u32[]{:S(2)}, u32[]{:S(2)}) collective-permute-start(bf16[1152,256]{1,0:T(8,128)(2,1)S(1)} %bitcast.15), channel_id=1, source_target_pairs={{0,1},{1,2},{2,3},{3,4},{4,5},{5,6},{6,7},{8,9},{9,10},{10,11},{11... | collective-permute-start | bytes 1769480 | tf_op jit(solution)/shard_map/ppermute | solution.py:203
  11.0 1.3 collective-permute-start.3
  12.9 1.3 copy.8
  14.2 5.4 %shard_map.77.st_ref = f32[8,768]{1,0:T(8,128)} custom-call(s32[1,1]{1,0:T(1,128)S(6)} %copy.10.ext_ref, bf16[3,2048,256]{2,1,0:T(8,128)(2,1)} %bitcast.9, bf16[3,2048,256]{2,1,0:T(8,128)(2,1)} %bitcast.11, f32[1,768]{1,0:T(1,128)} %bitcast.16), custom_call_target="tpu_custom_call" | custom-call | tf_op jit(solution)/shard_map/pallas_call | solution.py:209
  19.6 17.3 %shard_map.78.coef_ref = f32[8,768]{1,0:T(8,128)} custom-call(f32[8,768]{1,0:T(8,128)} %shard_map.77.st_ref, f32[1,768]{1,0:T(1,128)} %bitcast.17), custom_call_target="tpu_custom_call" | custom-call | tf_op jit(solution)/shard_map/pallas_call | solution.py:222
  37.0 9.3 %shard_map.79 = (bf16[3,3,2048,256]{3,2,1,0:T(8,128)(2,1)}, bf16[2304,256]{1,0:T(8,128)(2,1)}, bf16[2304,256]{1,0:T(8,128)(2,1)}) custom-call(s32[1,1]{1,0:T(1,128)S(6)} %copy.10.ext_ref, bf16[3,2048,256]{2,1,0:T(8,128)(2,1)} %bitcast.10, bf16[3,2048,256]{2,1,0:T(8,128)(2,1)} %bitcast.12, f32[8,768]{1,0:T(8,128)} %shard_map.78.coef_ref), custom_call_target="tpu_custom_call" | custom-call | tf_op jit(solution)/shard_map/pallas_call | solution.py:239
  46.2 0.0 collective-permute-done.2.before_ref
  46.2 0.0 copy-start.3
  46.3 0.0 collective-permute-done.3.after_ref
  46.3 0.0 copy-start.4
  46.3 0.8 copy-done.3
  47.1 0.2 copy-done.4
  47.3 14.5 %shard_map.81 = f32[3,3,3,256,256]{4,3,2,1,0:T(8,128)} custom-call(bf16[1152,256]{1,0:T(8,128)(2,1)} %copy-done.3, bf16[2048,256]{1,0:T(8,128)(2,1)} %bitcast.13, bf16[1152,256]{1,0:T(8,128)(2,1)} %copy-done.4, bf16[3,3,2048,256]{3,2,1,0:T(8,128)(2,1)} %get-tuple-element.7.g_ref), custom_call_target="tpu_custom_call" | custom-call | flops 7247757312 | bytes 20000000 | tf_op jit(solution)/shard_map/pallas_call | solution.py:260
  61.8 0.0 all-reduce.2.cloned.1.call-update
  61.8 1.2 copy-done.1
  63.1 1.4 collective-permute-start
  64.4 1.3 collective-permute-start.1
  65.7 2.0 collective-permute-done.before_ref
  67.8 3.4 %collective-permute-done.1.after_ref = bf16[2304,256]{1,0:T(8,128)(2,1)} collective-permute-done((bf16[2304,256]{1,0:T(8,128)(2,1)S(1)}, bf16[2304,256]{1,0:T(8,128)(2,1)}, u32[]{:S(2)}, u32[]{:S(2)}) %collective-permute-start.1) | collective-permute-done | bytes 1179680 | tf_op jit(solution)/shard_map/ppermute | solution.py:257
  71.2 20.7 %shard_map.80 = bf16[2048,256]{1,0:T(8,128)(2,1)} custom-call(bf16[2304,256]{1,0:T(8,128)(2,1)} %copy-done.2, bf16[2304,256]{1,0:T(8,128)(2,1)} %collective-permute-done.1.after_ref, bf16[3,3,2048,256]{3,2,1,0:T(8,128)(2,1)} %get-tuple-element.7.g_ref, bf16[3,3,3,256,256]{4,3,2,1,0:T(8,128)(2,1)} %w_ref.1), custom_call_target="tpu_custom_call" | custom-call | flops 7247757312 | bytes 20000000 | tf_op jit(solution)/shard_map/pallas_call | solution.py:276
  91.9 135.4 %all-reduce.2.cloned.1.call-done = f32[3,3,3,256,256]{4,3,2,1,0:T(8,128)} async-done(((f32[3,3,3,256,256]{4,3,2,1,0:T(8,128)}), f32[3,3,3,256,256]{4,3,2,1,0:T(8,128)}) %all-reduce.2.cloned.1.call-update) | async-done | bytes 7077904 | tf_op jit(solution)/shard_map/psum | solution.py:275
  227.3 6.7 %copy.11 = f32[3,3,3,256,256]{4,3,2,1,0:T(8,128)} copy(f32[3,3,3,256,256]{4,3,2,1,0:T(8,128)} %all-reduce.2.cloned.1.call-done) | data formatting | bytes 14155776
  (5 shorter events, 0.0 us)
Async XLA Ops:
  7.2 220.1 %all-reduce.2.cloned.1.call-start = ((), (), s32[]{:S(2)}) async-start(), calls=%async_computation | async-start | bytes 14155776 | tf_op jit(solution)/shard_map/psum | solution.py:275
  8.5 37.7 %collective-permute-start.2 = (bf16[1152,256]{1,0:T(8,128)(2,1)S(1)}, bf16[1152,256]{1,0:T(8,128)(2,1)S(1)}, u32[]{:S(2)}, u32[]{:S(2)}) collective-permute-start(bf16[1152,256]{1,0:T(8,128)(2,1)S(1)} %bitcast.15), channel_id=1, source_target_pairs={{0,1},{1,2},{2,3},{3,4},{4,5},{5,6},{6,7},{8,9},{9,10},{10,11},{11... | collective-permute-start | bytes 1769480 | tf_op jit(solution)/shard_map/ppermute | solution.py:203
  11.0 35.3 %collective-permute-start.3 = (bf16[1152,256]{1,0:T(8,128)(2,1)S(1)}, bf16[1152,256]{1,0:T(8,128)(2,1)S(1)}, u32[]{:S(2)}, u32[]{:S(2)}) collective-permute-start(bf16[1152,256]{1,0:T(8,128)(2,1)S(1)} %bitcast.14), channel_id=1, source_target_pairs={{1,0},{2,1},{3,2},{4,3},{5,4},{6,5},{7,6},{9,8},{10,9},{11,10},{12... | collective-permute-start | bytes 1769480 | tf_op jit(solution)/shard_map/ppermute | solution.py:204
  46.2 0.8 copy-start.3
  46.3 1.0 copy-start.4
  61.8 1.3 copy-start.1
  61.8 2.6 %copy-start = (bf16[2304,256]{1,0:T(8,128)(2,1)S(1)}, bf16[2304,256]{1,0:T(8,128)(2,1)}, u32[]{:S(2)}) copy-start(bf16[2304,256]{1,0:T(8,128)(2,1)} %get-tuple-element.6) | copy-start | bytes 3538948
  63.1 4.7 %collective-permute-start = (bf16[2304,256]{1,0:T(8,128)(2,1)S(1)}, bf16[2304,256]{1,0:T(8,128)(2,1)S(1)}, u32[]{:S(2)}, u32[]{:S(2)}) collective-permute-start(bf16[2304,256]{1,0:T(8,128)(2,1)S(1)} %copy-done.1), channel_id=1, source_target_pairs={{0,1},{1,2},{2,3},{3,4},{4,5},{5,6},{6,7},{8,9},{9,10},{10,11},{11... | collective-permute-start | bytes 3538952 | tf_op jit(solution)/shard_map/ppermute | solution.py:256
  64.4 6.8 %collective-permute-start.1 = (bf16[2304,256]{1,0:T(8,128)(2,1)S(1)}, bf16[2304,256]{1,0:T(8,128)(2,1)}, u32[]{:S(2)}, u32[]{:S(2)}) collective-permute-start(bf16[2304,256]{1,0:T(8,128)(2,1)S(1)} %copy-done), channel_id=1, source_target_pairs={{1,0},{2,1},{3,2},{4,3},{5,4},{6,5},{7,6},{9,8},{10,9},{11,10},{12... | collective-permute-start | bytes 3538952 | tf_op jit(solution)/shard_map/ppermute | solution.py:257
  67.7 3.4 %copy-start.2 = (bf16[2304,256]{1,0:T(8,128)(2,1)}, bf16[2304,256]{1,0:T(8,128)(2,1)S(1)}, u32[]{:S(2)}) copy-start(bf16[2304,256]{1,0:T(8,128)(2,1)S(1)} %collective-permute-done.before_ref) | copy-start | bytes 3538948
Sparse Core Ops, SparseCore 0:
  61.9 165.3 all-reduce.1

commit v2 on v1

--- a/solution.py
+++ b/solution.py
@@ -140,8 +140,9 @@
     out_ref[0, :, 0] = got.reshape(out_ref.shape[1], out_ref.shape[3], out_ref.shape[4])
 
 
-def input_terms(cols, rows, before_ref, after_ref, g_ref, w_ref, out_ref, ext, acc):
+def input_terms(cols, rows, before_ref, after_ref, g_ref, w_ref, k_ref, out_ref, k_out, ext, acc):
     branch, column = pl.program_id(0), pl.program_id(1)
+    k_out[...] = k_ref[...]
     ext[REACH * cols : (REACH + rows) * cols, :] = g_ref[0, 0]
     for k, rate in enumerate(RATES):
         for j in range(3):
@@ -182,6 +183,105 @@
         return 0
 
     lax.fori_loop(0, rows * cols // tile, block, 0)
+
+
+def reduce_all(n_space, n_dp, in_ref, out_ref, acc, rb, send, recv):
+    bits = n_space.bit_length() - 1
+    pieces = n_space * n_dp
+    streams = in_ref.shape[0]
+    space, dp = lax.axis_index("space"), lax.axis_index("dp")
+    mesh_id = pl.DeviceIdType.MESH
+
+    def bit_of(b):
+        return lax.rem(lax.div(space, 1 << b), 2)
+
+    def partner(b):
+        return {"space": space + (1 - 2 * bit_of(b)) * (1 << b)}
+
+    def peer(k):
+        return {"dp": lax.rem(dp + k, n_dp)}
+
+    others = [partner(b) for b in range(bits)] + [peer(k) for k in range(1, n_dp)]
+    barrier = pltpu.get_barrier_semaphore()
+    for other in others:
+        pl.semaphore_signal(barrier, inc=1, device_id=other, device_id_type=mesh_id)
+    pl.semaphore_wait(barrier, len(others))
+
+    def stages(st):
+        order = list(range(bits)) if st % 2 == 0 else [0] + list(range(bits - 1, 0, -1))
+        sem = 0
+
+        def copy(src, dst, k, device):
+            c = pltpu.make_async_remote_copy(
+                src_ref=src, dst_ref=dst, send_sem=send.at[st, k], recv_sem=recv.at[st, k],
+                device_id=device, device_id_type=mesh_id,
+            )
+            c.start()
+            return c
+
+        starts = []
+        base, room, size = 0, 0, pieces
+        for level, b in enumerate(order):
+            size = size // 2
+            mine = bit_of(b)
+            here, there = base + mine * size, base + (1 - mine) * size
+            src = in_ref if level == 0 else acc
+            c = copy(src.at[st, pl.ds(there, size)], rb.at[st, pl.ds(room, size)], sem, partner(b))
+            sem += 1
+            yield
+            c.wait()
+            dst = 0 if level == 0 else here
+
+            def add(i, _, src=src, here=here, dst=dst, room=room):
+                acc[st, dst + i] = src[st, here + i] + rb[st, room + i]
+                return 0
+
+            lax.fori_loop(0, size, add, 0)
+            starts.append((mine, size))
+            base = dst
+            room += size
+        whole = 0
+        ranges = []
+        for mine, size in starts:
+            whole = whole + mine * size
+            ranges.append((whole, size))
+        copies = []
+        for k in range(1, n_dp):
+            to = lax.rem(dp + k, n_dp)
+            copies.append(copy(acc.at[st, base + to], rb.at[st, room + k - 1], sem, peer(k)))
+            sem += 1
+        yield
+        total = acc[st, base + dp]
+        for k in range(1, n_dp):
+            copies[k - 1].wait()
+            total = total + rb[st, room + k - 1]
+        out_ref[st, whole + dp] = total
+        copies = []
+        for k in range(1, n_dp):
+            copies.append(copy(out_ref.at[st, whole + dp], out_ref.at[st, whole + dp], sem, peer(k)))
+            sem += 1
+        yield
+        for c in copies:
+            c.wait()
+        for (start, size), b in zip(ranges[::-1], order[::-1]):
+            span = out_ref.at[st, pl.ds(start, size)]
+            c = copy(span, span, sem, partner(b))
+            sem += 1
+            yield
+            c.wait()
+
+    running = []
+    waiting = [stages(st) for st in range(streams)]
+    while running or waiting:
+        alive = []
+        for run in running:
+            if next(run, 0) is None:
+                alive.append(run)
+        running = alive
+        if waiting:
+            run = waiting.pop(0)
+            next(run)
+            running.append(run)
 
 
 def vmem(shape=None, index=None):
@@ -272,8 +372,27 @@
         compiler_params=limit,
         cost_estimate=cost,
     )(f_before, feats, f_after, grads)
-    kernel_grad = lax.psum(terms, ("dp", "space"))
-    out = pl.pallas_call(
+    streams, pieces = 9, n_space * n_dp
+    per = 27 * chans // (streams * pieces)
+    shape = (streams, pieces, per, chans)
+    room = pieces - n_dp + n_dp - 1
+    sems = pltpu.SemaphoreType.DMA((streams, 2 * (n_space.bit_length() - 1 + n_dp - 1)))
+    reduced = pl.pallas_call(
+        functools.partial(reduce_all, n_space, n_dp),
+        in_specs=[vmem()],
+        out_specs=vmem(),
+        out_shape=jax.ShapeDtypeStruct(shape, F32),
+        scratch_shapes=[
+            pltpu.VMEM((streams, pieces // 2, per, chans), F32),
+            pltpu.VMEM((streams, room, per, chans), F32),
+            sems,
+            sems,
+        ],
+        compiler_params=pltpu.CompilerParams(
+            collective_id=1, has_side_effects=True, vmem_limit_bytes=60 * 1024 * 1024
+        ),
+    )(terms.reshape(shape)).reshape(streams, 3 * chans, chans)
+    out, kernel_grad = pl.pallas_call(
         functools.partial(input_terms, cols, rows),
         grid=(3, 3),
         in_specs=[
@@ -281,17 +400,24 @@
             vmem((BOTH * cols, chans), lambda b, j: (0, 0)),
             vmem((1, 1, pixels, chans), lambda b, j: (b, j, 0, 0)),
             vmem((1, 3, 1, chans, chans), lambda b, j: (b, 0, j, 0, 0)),
-        ],
-        out_specs=vmem((pixels, chans), lambda b, j: (0, 0)),
-        out_shape=jax.ShapeDtypeStruct((pixels, chans), BF16),
+            vmem((1, 3 * chans, chans), lambda b, j: (3 * b + j, 0, 0)),
+        ],
+        out_specs=[
+            vmem((pixels, chans), lambda b, j: (0, 0)),
+            vmem((1, 3 * chans, chans), lambda b, j: (3 * b + j, 0, 0)),
+        ],
+        out_shape=[
+            jax.ShapeDtypeStruct((pixels, chans), BF16),
+            jax.ShapeDtypeStruct((streams, 3 * chans, chans), F32),
+        ],
         scratch_shapes=[
             pltpu.VMEM((pixels + BOTH * cols, chans), BF16),
             pltpu.VMEM((pixels, chans), F32),
         ],
         compiler_params=limit,
         cost_estimate=cost,
-    )(g_before, g_after, grads, weight)
-    return out.reshape(1, rows, cols, chans), kernel_grad
+    )(g_before, g_after, grads, weight, reduced)
+    return out.reshape(1, rows, cols, chans), kernel_grad.reshape(weight.shape)
 
 
 def solution(mesh):

time: 242 us -> 190 us (0.79)
  waiting for transfers between devices: 141 us -> 0.01 us
  Pallas kernels: 67.2 us -> 177 us
  between operations: 14.8 us -> 1.37 us
  local copies, waits for them, and re-layouts: 11.6 us -> 4 us
    psum x1 -> x0, waiting for transfers between devices: 135 us -> none  [body(): kernel_grad = lax.psum(terms, ('dp', 'space'))]
    pallas_call x0 -> x1, Pallas kernels: none -> 109 us  [body(): pl.pallas_call(functools.partial(reduce_all, n_space, n_dp), in_specs=[vm...]
    unnamed x12 -> x5, local copies, waits for them, and re-layouts: 10.2 us -> 2.68 us
    ppermute x1, waiting for transfers between devices: 3.44 us -> 0.01 us  [body(): g_after = lax.ppermute(top, 'space', down_pairs)]
  transfers between devices with their start and end apart: 5 -> 4, of which waited for: 3 -> 0; matrix products, arithmetic and copies ran while one was open for 1% -> 1% of each run, Pallas kernels for 22% -> 82%
where the time goes in v2:
time: 190 us
  Pallas kernels  177 us (93%)
  starting transfers between devices  7.16 us (4%)
  local copies, waits for them, and re-layouts  4 us (2%)
    pallas_call x1, Pallas kernels, body(): pl.pallas_call(functools.partial(reduce_all, n_space, n_dp), in_specs=[vm...  109 us
    pallas_call x1, Pallas kernels, body(): pl.pallas_call(functools.partial(input_terms, cols, rows), grid=(3, 3), i...  22 us
    pallas_call x1, Pallas kernels, body(): pl.pallas_call(functools.partial(exchange, (('space', n_space), ('dp', n_...  17.1 us
    pallas_call x1, Pallas kernels, body(): pl.pallas_call(functools.partial(kernel_terms, cols, rows), grid=(3, 3),...  14.6 us
    pallas_call x1, Pallas kernels, body(): pl.pallas_call(functools.partial(gradients, cols, rows), grid=(3,), in_sp...  9.29 us
    pallas_call x1, Pallas kernels, body(): pl.pallas_call(functools.partial(local_stats, cols), grid=(3,), in_specs=...  4.86 us
  transfers between devices with their start and end apart: 4, of which 0 were waited for; matrix products, arithmetic and copies ran while one was open for 1% of the time, Pallas kernels for 82%

profile of v2, /device:TPU:0, one launch (start us, length us, event | category | flops | bytes accessed | tf_op | source)
XLA Modules:
  0.0 189.7 jit_solution(14551762022944809569)
XLA Ops:
  0.6 1.3 fusion
  2.0 3.2 %collective-permute-start.2 = (bf16[1152,256]{1,0:T(8,128)(2,1)S(1)}, bf16[1152,256]{1,0:T(8,128)(2,1)}, u32[]{:S(2)}, u32[]{:S(2)}) collective-permute-start(bf16[1152,256]{1,0:T(8,128)(2,1)S(1)} %bitcast.20), channel_id=1, source_target_pairs={{0,1},{1,2},{2,3},{3,4},{4,5},{5,6},{6,7},{8,9},{9,10},{10,11},{11... | collective-permute-start | bytes 1769480 | tf_op jit(solution)/shard_map/ppermute | solution.py:303
  5.2 1.3 collective-permute-start.3
  7.1 1.3 copy.8
  8.4 4.9 %shard_map.77.st_ref = f32[8,768]{1,0:T(8,128)} custom-call(s32[1,1]{1,0:T(1,128)S(6)} %copy.9.ext_ref, bf16[3,2048,256]{2,1,0:T(8,128)(2,1)} %bitcast.12, bf16[3,2048,256]{2,1,0:T(8,128)(2,1)} %bitcast.14, f32[1,768]{1,0:T(1,128)} %bitcast.21), custom_call_target="tpu_custom_call" | custom-call | tf_op jit(solution)/shard_map/pallas_call | solution.py:309
  13.3 17.1 %shard_map.78.coef_ref = f32[8,768]{1,0:T(8,128)} custom-call(f32[8,768]{1,0:T(8,128)} %shard_map.77.st_ref, f32[1,768]{1,0:T(1,128)} %bitcast.22), custom_call_target="tpu_custom_call" | custom-call | tf_op jit(solution)/shard_map/pallas_call | solution.py:322
  30.4 9.3 %shard_map.79 = (bf16[3,3,2048,256]{3,2,1,0:T(8,128)(2,1)}, bf16[2304,256]{1,0:T(8,128)(2,1)}, bf16[2304,256]{1,0:T(8,128)(2,1)}) custom-call(s32[1,1]{1,0:T(1,128)S(6)} %copy.9.ext_ref, bf16[3,2048,256]{2,1,0:T(8,128)(2,1)} %bitcast.13, bf16[3,2048,256]{2,1,0:T(8,128)(2,1)} %bitcast.15, f32[8,768]{1,0:T(8,128)} %shard_map.78.coef_ref), custom_call_target="tpu_custom_call" | custom-call | tf_op jit(solution)/shard_map/pallas_call | solution.py:339
  39.7 1.4 collective-permute-start
  41.1 1.3 collective-permute-start.1
  42.4 0.0 collective-permute-done.2.before_ref
  42.4 0.0 collective-permute-done.3.after_ref
  42.4 14.6 %shard_map.80 = f32[3,3,3,256,256]{4,3,2,1,0:T(8,128)} custom-call(bf16[1152,256]{1,0:T(8,128)(2,1)} %collective-permute-done.2.before_ref, bf16[2048,256]{1,0:T(8,128)(2,1)} %bitcast.18, bf16[1152,256]{1,0:T(8,128)(2,1)} %collective-permute-done.3.after_ref, bf16[3,3,2048,256]{3,2,1,0:T(8,128)(2,1)} %get-tuple-element.9.g_ref), custom_call_target="tpu_custom_call" | custom-call | flops 7247757312 | bytes 20000000 | tf_op jit(solution)/shard_map/pallas_call | solution.py:360
  56.9 109.3 %shard_map.81 = f32[9,32,24,256]{3,2,1,0:T(8,128)} custom-call(f32[9,32,24,256]{3,2,1,0:T(8,128)} %bitcast.17), custom_call_target="tpu_custom_call" | custom-call | tf_op jit(solution)/shard_map/pallas_call | solution.py:380
  166.3 0.0 collective-permute-done.before_ref
  166.3 0.0 copy-start
  166.3 0.0 collective-permute-done.1.after_ref
  166.3 0.0 copy-start.1
  166.3 1.0 copy-done
  167.3 0.4 copy-done.1
  167.7 22.0 %shard_map.82 = (bf16[2048,256]{1,0:T(8,128)(2,1)}, f32[9,768,256]{2,1,0:T(8,128)}) custom-call(bf16[2304,256]{1,0:T(8,128)(2,1)} %copy-done, bf16[2304,256]{1,0:T(8,128)(2,1)} %copy-done.1, bf16[3,3,2048,256]{3,2,1,0:T(8,128)(2,1)} %get-tuple-element.9.g_ref, bf16[3,3,3,256,256]{4,3,2,1,0:T(8,128)(2,1)} %w_ref.1, f32[9,768,256]{2,1,0:T(8,128)} %bitcast.16), custom_call_target="tpu_custom_call" | custom-call | flops 7247757312 | bytes 20000000 | tf_op jit(solution)/shard_map/pallas_call | solution.py:395
Async XLA Ops:
  2.0 40.4 %collective-permute-start.2 = (bf16[1152,256]{1,0:T(8,128)(2,1)S(1)}, bf16[1152,256]{1,0:T(8,128)(2,1)}, u32[]{:S(2)}, u32[]{:S(2)}) collective-permute-start(bf16[1152,256]{1,0:T(8,128)(2,1)S(1)} %bitcast.20), channel_id=1, source_target_pairs={{0,1},{1,2},{2,3},{3,4},{4,5},{5,6},{6,7},{8,9},{9,10},{10,11},{11... | collective-permute-start | bytes 1769480 | tf_op jit(solution)/shard_map/ppermute | solution.py:303
  5.2 37.2 %collective-permute-start.3 = (bf16[1152,256]{1,0:T(8,128)(2,1)S(1)}, bf16[1152,256]{1,0:T(8,128)(2,1)}, u32[]{:S(2)}, u32[]{:S(2)}) collective-permute-start(bf16[1152,256]{1,0:T(8,128)(2,1)S(1)} %bitcast.19), channel_id=1, source_target_pairs={{1,0},{2,1},{3,2},{4,3},{5,4},{6,5},{7,6},{9,8},{10,9},{11,10},{12... | collective-permute-start | bytes 1769480 | tf_op jit(solution)/shard_map/ppermute | solution.py:304
  39.7 126.6 %collective-permute-start = (bf16[2304,256]{1,0:T(8,128)(2,1)}, bf16[2304,256]{1,0:T(8,128)(2,1)S(1)}, u32[]{:S(2)}, u32[]{:S(2)}) collective-permute-start(bf16[2304,256]{1,0:T(8,128)(2,1)} %get-tuple-element.7), channel_id=1, source_target_pairs={{0,1},{1,2},{2,3},{3,4},{4,5},{5,6},{6,7},{8,9},{9,10},{10,11},{11... | collective-permute-start | bytes 3538952 | tf_op jit(solution)/shard_map/ppermute | solution.py:356
  41.1 125.2 %collective-permute-start.1 = (bf16[2304,256]{1,0:T(8,128)(2,1)}, bf16[2304,256]{1,0:T(8,128)(2,1)S(1)}, u32[]{:S(2)}, u32[]{:S(2)}) collective-permute-start(bf16[2304,256]{1,0:T(8,128)(2,1)} %get-tuple-element.8), channel_id=1, source_target_pairs={{1,0},{2,1},{3,2},{4,3},{5,4},{6,5},{7,6},{9,8},{10,9},{11,10},{12... | collective-permute-start | bytes 3538952 | tf_op jit(solution)/shard_map/ppermute | solution.py:357
  166.3 1.1 copy-start
  166.3 1.4 copy-start.1
